TPU v7x, 32 devices: a whole 2x2x4 slice. The times are simulated.
32 devices in a mesh: chan: 8 (over y, x, core), win: 4 (over z).
Axes of the slice: x: 2, y: 2, z: 4, core: 2. Of those that a mesh axis runs over, the one named last changes fastest.
Arguments:
- records: float32 [16, 1024, 256], P('win', 'chan'), may hold values from -180 to 180
- sources: int32 [32], replicated, may hold values from 0 to 255, as said below
Outputs:
- correlations: float32 [32, 256, 256], P('win', None, 'chan')
Inputs may be any that keep to these rules, and one draw needn't show every extreme that they name: `sources`: source s is one of the channels s * 8 to (s + 1) * 8 - 1; the first source is channel 0 and the last is channel 256 - 1.
All inputs are finite; a program needn't handle non-finite values.
Results may differ from a plain program's by a relative error of at most 0.00022.
Values sent between devices are 32-bit elements; how exact they have to be, the bound alone decides.
A program may use at most 64 MiB of HBM per device.

v0:
```python
import math
import jax
import jax.numpy as jnp
from jax import lax
from jax.sharding import PartitionSpec as P

HIGHEST = lax.Precision.HIGHEST
AMPLITUDE_FLOOR = 0.25
WHITE_EPSILON = 1e-06


def fourier_table(length):
    freq_count = length // 2
    freqs = jnp.arange(freq_count, dtype=jnp.int32)[:, None]
    sample_index = jnp.arange(length, dtype=jnp.int32)[None, :]
    angles = (freqs * sample_index % length).astype(jnp.float32) * (2.0 * math.pi / length)
    return jnp.concatenate([jnp.cos(angles), -jnp.sin(angles)], axis=0)


def band_table(freq_count, reach):
    rows_index = jnp.arange(freq_count, dtype=jnp.int32)[:, None]
    cols_index = jnp.arange(freq_count, dtype=jnp.int32)[None, :]
    return (jnp.abs(rows_index - cols_index) <= reach).astype(jnp.float32)


def inverse_table(length, lag_count, first_bin, bin_count, factor):
    freqs = first_bin + jnp.arange(bin_count, dtype=jnp.int32)
    lag_index = jnp.arange(lag_count, dtype=jnp.int32) - lag_count // 2
    angles = (lag_index[:, None] * freqs[None, :] % length).astype(jnp.float32) * (
        2.0 * math.pi / length
    )
    weights = jnp.where(freqs == 0, 1.0, 2.0).astype(jnp.float32)[None, :] * factor
    return jnp.concatenate([weights * jnp.cos(angles), -weights * jnp.sin(angles)], axis=1)


def running_level(padded, time_count, window_span):
    window_total = padded.shape[0]
    chans = padded.shape[2]
    running = jnp.concatenate(
        [jnp.zeros((window_total, 1, chans), jnp.float32), jnp.cumsum(jnp.abs(padded), axis=1)],
        axis=1,
    )
    return (running[:, window_span:] - running[:, :time_count]) / window_span


def local(records, sources):
    chan_count = lax.axis_size("chan")
    local_windows, local_time, all_channels = records.shape
    length = local_time * chan_count
    freq_count = length // 2
    chan_width = all_channels // chan_count
    half_width = min(16, local_time)
    smooth_reach = length // 32
    window_span = 2 * half_width + 1
    lag_count = length // 4
    forward = fourier_table(length)
    band_matrix = band_table(freq_count, smooth_reach)
    pieces = lax.all_to_all(records, "chan", split_axis=2, concat_axis=1, tiled=True)
    padded = jnp.pad(pieces, ((0, 0), (half_width, half_width), (0, 0)))
    amplitude = running_level(padded, length, window_span)
    whiten_pieces = pieces / jnp.maximum(amplitude, AMPLITUDE_FLOOR)
    spectrum = jnp.einsum("kt,wtc->wkc", forward, whiten_pieces, precision=HIGHEST)
    real_part = spectrum[:, :freq_count]
    imag_part = spectrum[:, freq_count:]
    magnitude = jnp.sqrt(real_part * real_part + imag_part * imag_part)
    smoothed = (
        jnp.einsum("jk,wkc->wjc", band_matrix, magnitude, precision=HIGHEST)
        / (2 * smooth_reach + 1)
        + WHITE_EPSILON
    )
    whitened = jnp.stack([real_part / smoothed, imag_part / smoothed], axis=1)
    band_data = lax.all_to_all(whitened, "win", split_axis=2, concat_axis=0, tiled=True)
    total_windows = band_data.shape[0]
    band_count = band_data.shape[2]
    source_count = sources.shape[0]
    chan_index = lax.axis_index("chan")
    channel_ids = jnp.arange(chan_width, dtype=jnp.int32)
    per_device = source_count // chan_count
    owned_local = (
        lax.dynamic_slice_in_dim(sources, chan_index * per_device, per_device)
        - chan_index * chan_width
    )
    selector = (owned_local[:, None] == channel_ids[None, :]).astype(jnp.float32)
    chosen = jnp.einsum("sc,wafc->wafs", selector, band_data, precision=HIGHEST)
    spectra = lax.all_gather(chosen, "chan", axis=3, tiled=True)
    source_real = spectra[:, 0]
    source_imag = spectra[:, 1]
    white_real = band_data[:, 0]
    white_imag = band_data[:, 1]
    cross_real = jnp.einsum(
        "wfs,wfc->fsc", source_real, white_real, precision=HIGHEST
    ) + jnp.einsum("wfs,wfc->fsc", source_imag, white_imag, precision=HIGHEST)
    cross_imag = jnp.einsum(
        "wfs,wfc->fsc", source_real, white_imag, precision=HIGHEST
    ) - jnp.einsum("wfs,wfc->fsc", source_imag, white_real, precision=HIGHEST)
    stacked = jnp.stack([cross_real, cross_imag])
    factor = 1.0 / math.sqrt(total_windows * freq_count)
    band_start = lax.axis_index("win") * band_count
    band_table_part = inverse_table(length, lag_count, band_start, band_count, factor).reshape(
        lag_count, 2, band_count
    )
    return lax.psum_scatter(
        jnp.einsum("tak,aksc->stc", band_table_part, stacked, precision=HIGHEST),
        "win",
        scatter_dimension=0,
        tiled=True,
    )


def solution(mesh):
    placed = (P("win", "chan", None), P())
    return jax.shard_map(
        local, mesh=mesh, in_specs=placed, out_specs=P("win", None, "chan"), check_vma=False
    )
```

profile of v0, /device:TPU:0, one launch (start us, length us, event | category | flops | bytes accessed | tf_op | source)
XLA Modules:
  0.0 168.4 jit_solution(1420910097086612107)
XLA Ops:
  6.5 2.1 %copy.58 = f32[4,128,256]{1,0,2:T(4,128)} copy(f32[4,128,256]{2,1,0:T(8,128)} %param.2) | data formatting | bytes 1048576 | tf_op args[0]
  8.6 5.2 %all-to-all-start = ((f32[4,128,256]{1,0,2:T(4,128)}), f32[4,128,256]{1,0,2:T(4,128)S(1)}, u32[]{:S(2)}, u32[]{:S(2)}) async-start(f32[4,128,256]{1,0,2:T(4,128)} %copy.58), calls=%async_computation | async-start | bytes 1048576 | tf_op jit(solution)/shard_map/all_to_all | solution.py:58
  13.8 9.2 %sine_negate_fusion = (f32[512,1024]{1,0:T(8,128)}, f32[512,1024]{1,0:T(8,128)}) fusion(), kind=kLoop, calls=%fused_computation.15 | loop fusion | flops 7864320 | bytes 4194304 | tf_op jit(solution)/shard_map/neg | solution.py:17
  23.0 0.5 all-to-all-done
  23.6 0.2 abs_bitcast_fusion
  23.9 0.1 reshape.194
  24.0 36.3 %reduce-window.6 = f32[4,32,9,128]{3,2,1,0:T(8,128)S(1)} reduce-window(f32[4,32,9,128]{3,2,1,0:T(8,128)S(1)} %reshape.194, f32[]{:T(128)} %constant.22.clone.1), window={size=1x1x1x128 pad=0_0x0_0x0_0x127_0}, to_apply=%region_0.1 | reduce-window | flops 18726912 | bytes 1179652 | tf_op jit(solution)/shard_map/reduce-window
  60.3 0.3 slice.45
  60.6 0.4 copy.61
  61.0 0.1 copy.62
  61.1 0.3 broadcast_add_fusion
  61.4 0.1 reduce_window_sum.16
  61.5 6.6 %fusion.14 = f32[4,1024,32]{1,2,0:T(8,128)S(1)} fusion(f32[512,1024]{1,0:T(8,128)} %get-tuple-element.13, f32[512,1024]{1,0:T(8,128)} %get-tuple-element.14, f32[4,1056,32]{1,2,0:T(8,128)S(1)} %bitcast.87, f32[4,1152,32]{1,2,0:T(8,128)S(1)} %bitcast.86, f32[4,8,4,8,128]{4,3,2,1,0:T(8,128)S(1)} %bitcast.84), kind=kOutput, calls=%fused_computation.20 | convolution fusion | flops 1612185600 | bytes 6356992 | tf_op jit(solution)/shard_map/kt,wtc->wkc/dot_general | solution.py:62
  68.1 0.7 divide_bitcast_fusion.1
  68.9 1.1 copy.63
  69.9 0.0 copy-start.2
  70.0 2.1 %reshape.201 = f32[4,1,32768]{2,1,0:T(1,128)} reshape(f32[512,2,4,32]{3,2,1,0:T(4,128)S(1)} %bitcast.79) | data formatting | bytes 1048576
  72.0 4.9 %all-to-all-start.1 = ((f32[4,1,32768]{2,1,0:T(1,128)}), f32[4,1,32768]{2,1,0:T(1,128)S(1)}, u32[]{:S(2)}, u32[]{:S(2)}) async-start(f32[4,1,32768]{2,1,0:T(1,128)} %reshape.201), calls=%async_computation.1 | async-start | bytes 1048576 | tf_op jit(solution)/shard_map/all_to_all | solution.py:72
  76.9 0.0 reduce-scatter.2.cloned.1.call-start
  76.9 0.0 copy-done.2
  76.9 0.1 dynamic-slice_subtract_fusion
  77.0 1.3 cosine_multiply_fusion
  78.2 13.3 %all-to-all-done.1 = f32[4,1,32768]{2,1,0:T(1,128)S(1)} async-done(((f32[4,1,32768]{2,1,0:T(1,128)}), f32[4,1,32768]{2,1,0:T(1,128)S(1)}, u32[]{:S(2)}, u32[]{:S(2)}) %all-to-all-start.1) | async-done | bytes 524320 | tf_op jit(solution)/shard_map/all_to_all | solution.py:72
  91.5 0.5 broadcast.245
  92.0 2.1 %reduce = f32[4,32768]{1,0:T(4,128)S(1)} reduce(f32[4,1,32768]{2,1,0:T(1,128)S(1)} %all-to-all-done.1, f32[]{:T(128)} %broadcast.245), dimensions={1}, to_apply=%all_to_all.30.reduce_sub_computation | reduce | bytes 1048580 | tf_op jit(solution)/shard_map/all_to_all | solution.py:72
  94.2 1.1 reshape.202
  95.3 0.8 copy.64
  96.2 0.3 fusion.49
  96.5 10.0 %all_gather.3 = f32[16,2,128,32]{2,0,1,3:T(8,128)S(1)} all-gather(f32[16,2,128,4]{2,0,1,3:T(8,128)S(1)} %copy.65), channel_id=1, replica_groups=mesh['chan'=8,'win'=4] {'chan'}, dimensions={3}, use_global_device_ids=true | all-gather | bytes 589824 | tf_op jit(solution)/shard_map/all_gather | solution.py:85
  106.5 0.7 fusion.60
  107.2 0.5 copy.77
  107.7 0.5 copy.67
  108.2 1.5 copy.78
  109.7 1.4 copy.69
  111.1 0.0 copy-start
  111.1 3.6 %fusion.21 = f32[128,32,32]{2,1,0:T(8,128)S(1)} fusion(f32[16,128,32]{2,0,1:T(8,128)S(1)} %copy.67, f32[16,1,128,32]{3,0,2,1:T(8,128)S(1)} %copy.77), kind=kOutput, calls=%fused_computation.28 | convolution fusion | flops 25165824 | bytes 1048576 | tf_op jit(solution)/shard_map/wfs,wfc->fsc/dot_general | solution.py:90
  114.7 0.0 copy-done
  114.7 3.6 %fusion.19 = f32[128,32,32]{2,1,0:T(8,128)S(1)} fusion(f32[16,128,32]{2,0,1:T(8,128)S(1)} %copy-done, f32[16,1,128,32]{3,0,2,1:T(8,128)S(1)} %copy.77), kind=kOutput, calls=%fused_computation.26 | convolution fusion | flops 25165824 | bytes 1048576 | tf_op jit(solution)/shard_map/wfs,wfc->fsc/dot_general | solution.py:93
  118.4 3.9 %add_bitcast_fusion = f32[1,128,32,32]{3,2,1,0:T(8,128)S(1)} fusion(f32[128,32,32]{2,1,0:T(8,128)S(1)} %fusion.21, f32[16,128,32]{2,0,1:T(8,128)S(1)} %copy-done, f32[16,1,128,32]{3,0,2,1:T(8,128)S(1)} %copy.78), kind=kOutput, calls=%fused_computation.14 | convolution fusion | flops 25296896 | bytes 1572864 | tf_op jit(solution)/shard_map/wfs,wfc->fsc/dot_general | solution.py:92
  122.3 3.7 %subtract_bitcast_fusion = f32[1,128,32,32]{3,2,1,0:T(8,128)S(1)} fusion(f32[128,32,32]{2,1,0:T(8,128)S(1)} %fusion.19, f32[16,128,32]{2,0,1:T(8,128)S(1)} %copy.67, f32[16,1,128,32]{3,0,2,1:T(8,128)S(1)} %copy.78), kind=kOutput, calls=%fused_computation.13 | convolution fusion | flops 25296896 | bytes 1572864 | tf_op jit(solution)/shard_map/wfs,wfc->fsc/dot_general | solution.py:95
  126.0 0.0 copy-start.1
  126.0 0.6 pad_maximum_fusion
  126.6 0.3 copy-done.1
  126.9 9.1 %fusion.11 = f32[32,256,32]{1,2,0:T(8,128)} fusion(f32[2,128,32,32]{3,2,1,0:T(8,128)S(1)} %pad_maximum_fusion, f32[256,1,128]{2,0,1:T(8,128)S(1)} %copy-done.1, f32[256,1,128]{2,0,1:T(8,128)S(1)} %get-tuple-element.11), kind=kOutput, calls=%fused_computation.19 | convolution fusion | flops 805371904 | bytes 2359296 | tf_op jit(solution)/shard_map/tak,aksc->stc/dot_general | solution.py:103
  136.0 0.0 reduce-scatter.2.cloned.1.call-update
  136.0 25.6 %reduce-scatter.2.cloned.1.call-done = f32[8,256,32]{1,2,0:T(8,128)} async-done(((f32[32,256,32]{1,2,0:T(8,128)}), f32[8,256,32]{1,2,0:T(8,128)}) %reduce-scatter.2.cloned.1.call-update) | async-done | bytes 262160 | tf_op jit(solution)/shard_map/reduce_scatter | solution.py:102
  (11 shorter events, 0.2 us)
Async XLA Ops:
  8.6 14.9 %all-to-all-start = ((f32[4,128,256]{1,0,2:T(4,128)}), f32[4,128,256]{1,0,2:T(4,128)S(1)}, u32[]{:S(2)}, u32[]{:S(2)}) async-start(f32[4,128,256]{1,0,2:T(4,128)} %copy.58), calls=%async_computation | async-start | bytes 1048576 | tf_op jit(solution)/shard_map/all_to_all | solution.py:58
  69.9 6.9 %copy-start.2 = (s32[32]{0:T(128)S(1)}, s32[32]{0:T(128)}, u32[]{:S(2)}) copy-start(s32[32]{0:T(128)} %param.3) | copy-start | bytes 388
  72.0 19.5 %all-to-all-start.1 = ((f32[4,1,32768]{2,1,0:T(1,128)}), f32[4,1,32768]{2,1,0:T(1,128)S(1)}, u32[]{:S(2)}, u32[]{:S(2)}) async-start(f32[4,1,32768]{2,1,0:T(1,128)} %reshape.201), calls=%async_computation.1 | async-start | bytes 1048576 | tf_op jit(solution)/shard_map/all_to_all | solution.py:72
  76.9 84.7 %reduce-scatter.2.cloned.1.call-start = ((), (), s32[]{:S(2)}) async-start(), calls=%async_computation.3 | async-start | bytes 1310720 | tf_op jit(solution)/shard_map/reduce_scatter | solution.py:102
  111.1 3.6 %copy-start = (f32[16,128,32]{2,0,1:T(8,128)S(1)}, f32[16,128,32]{2,0,1:T(8,128)}, u32[]{:S(2)}) copy-start(f32[16,128,32]{2,0,1:T(8,128)} %copy.69) | copy-start | bytes 786436
  126.0 0.9 copy-start.1
Sparse Core Ops, SparseCore 0:
  136.1 25.3 reduce-scatter.1
where the time goes:
time: 169 us; the launch traced here: 168 us
  other arithmetic  50.1 us (30%)
  waiting for transfers between devices  39.4 us (23%)
  matrix products  31.5 us (19%)
  local copies, waits for them, and re-layouts  13.8 us (8%)
  between operations  13.6 us (8%)
  starting transfers between devices  10.1 us (6%)
  blocking collectives  9.97 us (6%)
    another operation x3, other arithmetic  36.6 us
    reduce_scatter x1, waiting for transfers between devices, local(): lax.psum_scatter(jnp.einsum('tak,aksc->stc', band_table_part, stacked, pr...  25.6 us
    all_to_all x1, waiting for transfers between devices, local(): lax.all_to_all(whitened, 'win', split_axis=2, concat_axis=0, tiled=True)  13.3 us
    all_gather x1, blocking collectives, local(): spectra = lax.all_gather(chosen, 'chan', axis=3, tiled=True)  9.97 us
    neg x1, other arithmetic, fourier_table(): return jnp.concatenate([jnp.cos(angles), -jnp.sin(angles)], axis=0)  9.19 us
    dot_general x1, matrix products, local(): jnp.einsum('tak,aksc->stc', band_table_part, stacked, precision=HIGHEST)  9.09 us
    unnamed x11, local copies, waits for them, and re-layouts  7.61 us
    dot_general x1, matrix products, local(): jnp.einsum('kt,wtc->wkc', forward, whiten_pieces, precision=HIGHEST)  6.57 us
  transfers between devices with their start and end apart: 3, of which 3 were waited for; matrix products, arithmetic and copies ran while one was open for 6% of the time, Pallas kernels for 0%

commit v1 on v0

--- a/solution.py
+++ b/solution.py
@@ -82,7 +82,9 @@
     )
     selector = (owned_local[:, None] == channel_ids[None, :]).astype(jnp.float32)
     chosen = jnp.einsum("sc,wafc->wafs", selector, band_data, precision=HIGHEST)
-    spectra = lax.all_gather(chosen, "chan", axis=3, tiled=True)
+    spectra = jnp.concatenate(
+        lax.all_to_all(jnp.stack([chosen] * lax.axis_size("chan")), "chan", 0, 0), axis=3
+    )
     source_real = spectra[:, 0]
     source_imag = spectra[:, 1]
     white_real = band_data[:, 0]

time: 169 us -> 171 us (1.012)
  blocking collectives: 9.97 us -> 0 us
  waiting for transfers between devices: 39.4 us -> 46.9 us
  starting transfers between devices: 10.1 us -> 14.1 us
    all_gather x1 -> x0, blocking collectives: 9.97 us -> none  [local(): spectra = lax.all_gather(chosen, 'chan', axis=3, tiled=True)]
    all_to_all x0 -> x1, waiting for transfers between devices: none -> 7.18 us  [local(): lax.all_to_all(jnp.stack([chosen] * lax.axis_size('chan')), 'chan', 0, 0)]
    all_to_all x0 -> x1, starting transfers between devices: none -> 3.81 us  [local(): lax.all_to_all(jnp.stack([chosen] * lax.axis_size('chan')), 'chan', 0, 0)]
  transfers between devices with their start and end apart: 3 -> 4, of which waited for: 3 -> 4; matrix products, arithmetic and copies ran while one was open for 6% -> 7% of each run, Pallas kernels for 0% -> 0%
where the time goes in v1:
time: 171 us
  other arithmetic  50.1 us (29%)
  waiting for transfers between devices  46.9 us (27%)
  matrix products  32.8 us (19%)
  starting transfers between devices  14.1 us (8%)
  between operations  13.6 us (8%)
  local copies, waits for them, and re-layouts  13 us (8%)
    another operation x3, other arithmetic  36.6 us
    reduce_scatter x1, waiting for transfers between devices, local(): lax.psum_scatter(jnp.einsum('tak,aksc->stc', band_table_part, stacked, pr...  24.7 us
    all_to_all x1, waiting for transfers between devices, local(): lax.all_to_all(whitened, 'win', split_axis=2, concat_axis=0, tiled=True)  14.5 us
    neg x1, other arithmetic, fourier_table(): return jnp.concatenate([jnp.cos(angles), -jnp.sin(angles)], axis=0)  9.17 us
    dot_general x1, matrix products, local(): jnp.einsum('tak,aksc->stc', band_table_part, stacked, precision=HIGHEST)  9.1 us
    unnamed x11, local copies, waits for them, and re-layouts  7.53 us
    all_to_all x1, waiting for transfers between devices, local(): lax.all_to_all(jnp.stack([chosen] * lax.axis_size('chan')), 'chan', 0, 0)  7.18 us
    dot_general x1, matrix products, local(): jnp.einsum('kt,wtc->wkc', forward, whiten_pieces, precision=HIGHEST)  6.56 us
  transfers between devices with their start and end apart: 4, of which 4 were waited for; matrix products, arithmetic and copies ran while one was open for 7% of the time, Pallas kernels for 0%

profile of v1, /device:TPU:0, one launch (start us, length us, event | category | flops | bytes accessed | tf_op | source)
XLA Modules:
  0.0 170.6 jit_solution(17390002214347085035)
XLA Ops:
  6.5 2.0 %copy.54 = f32[4,128,256]{1,0,2:T(4,128)} copy(f32[4,128,256]{2,1,0:T(8,128)} %param.2) | data formatting | bytes 1048576 | tf_op args[0]
  8.6 5.2 %all-to-all-start = ((f32[4,128,256]{1,0,2:T(4,128)}), f32[4,128,256]{1,0,2:T(4,128)S(1)}, u32[]{:S(2)}, u32[]{:S(2)}) async-start(f32[4,128,256]{1,0,2:T(4,128)} %copy.54), calls=%async_computation | async-start | bytes 1048576 | tf_op jit(solution)/shard_map/all_to_all | solution.py:58
  13.8 9.2 %sine_negate_fusion = (f32[512,1024]{1,0:T(8,128)}, f32[512,1024]{1,0:T(8,128)}) fusion(), kind=kLoop, calls=%fused_computation.15 | loop fusion | flops 7864320 | bytes 4194304 | tf_op jit(solution)/shard_map/neg | solution.py:17
  22.9 0.5 all-to-all-done
  23.6 0.2 abs_bitcast_fusion
  23.9 0.1 reshape.202
  24.0 36.3 %reduce-window.6 = f32[4,32,9,128]{3,2,1,0:T(8,128)S(1)} reduce-window(f32[4,32,9,128]{3,2,1,0:T(8,128)S(1)} %reshape.202, f32[]{:T(128)} %constant.22.clone.1), window={size=1x1x1x128 pad=0_0x0_0x0_0x127_0}, to_apply=%region_0.1 | reduce-window | flops 18726912 | bytes 1179652 | tf_op jit(solution)/shard_map/reduce-window
  60.2 0.3 slice.45
  60.6 0.4 copy.57
  61.0 0.1 copy.58
  61.1 0.3 broadcast_add_fusion
  61.4 0.1 reduce_window_sum.16
  61.5 6.6 %fusion.14 = f32[4,1024,32]{1,2,0:T(8,128)S(1)} fusion(f32[512,1024]{1,0:T(8,128)} %get-tuple-element.13, f32[512,1024]{1,0:T(8,128)} %get-tuple-element.14, f32[4,1056,32]{1,2,0:T(8,128)S(1)} %bitcast.91, f32[4,1152,32]{1,2,0:T(8,128)S(1)} %bitcast.90, f32[4,8,4,8,128]{4,3,2,1,0:T(8,128)S(1)} %bitcast.87), kind=kOutput, calls=%fused_computation.20 | convolution fusion | flops 1612185600 | bytes 6356992 | tf_op jit(solution)/shard_map/kt,wtc->wkc/dot_general | solution.py:62
  68.1 0.7 divide_bitcast_fusion.1
  68.8 1.1 copy.59
  69.9 0.0 copy-start.2
  69.9 2.1 %reshape.211 = f32[4,1,32768]{2,1,0:T(1,128)} reshape(f32[512,2,4,32]{3,2,1,0:T(4,128)S(1)} %bitcast.82) | data formatting | bytes 1048576
  72.0 4.9 %all-to-all-start.1 = ((f32[4,1,32768]{2,1,0:T(1,128)}), f32[4,1,32768]{2,1,0:T(1,128)S(1)}, u32[]{:S(2)}, u32[]{:S(2)}) async-start(f32[4,1,32768]{2,1,0:T(1,128)} %reshape.211), calls=%async_computation.1 | async-start | bytes 1048576 | tf_op jit(solution)/shard_map/all_to_all | solution.py:72
  76.9 0.0 copy-done.2
  76.9 0.1 dynamic-slice_subtract_fusion
  77.0 14.5 %all-to-all-done.1 = f32[4,1,32768]{2,1,0:T(1,128)S(1)} async-done(((f32[4,1,32768]{2,1,0:T(1,128)}), f32[4,1,32768]{2,1,0:T(1,128)S(1)}, u32[]{:S(2)}, u32[]{:S(2)}) %all-to-all-start.1) | async-done | bytes 524320 | tf_op jit(solution)/shard_map/all_to_all | solution.py:72
  91.5 0.5 broadcast.247
  92.0 2.1 %reduce = f32[4,32768]{1,0:T(4,128)S(1)} reduce(f32[4,1,32768]{2,1,0:T(1,128)S(1)} %all-to-all-done.1, f32[]{:T(128)} %broadcast.247), dimensions={1}, to_apply=%all_to_all.33.reduce_sub_computation | reduce | bytes 1048580 | tf_op jit(solution)/shard_map/all_to_all | solution.py:72
  94.1 1.1 reshape.212
  95.3 0.8 copy.60
  96.1 0.3 fusion.49
  96.4 0.8 stack.32
  97.2 3.8 %all-to-all-start.2 = ((f32[8,16,2,128,4]{3,1,4,2,0:T(8,128)}), f32[8,16,2,128,4]{3,1,4,2,0:T(8,128)S(1)}, u32[]{:S(2)}, u32[]{:S(2)}) async-start(f32[8,16,2,128,4]{3,1,4,2,0:T(8,128)} %stack.32), calls=%async_computation.2 | async-start | bytes 1048576 | tf_op jit(solution)/shard_map/all_to_all | solution.py:86
  101.0 0.2 reduce-scatter.2.cloned.1.call-start
  101.3 1.3 cosine_multiply_fusion
  102.6 0.5 copy.64
  103.1 0.5 copy.66
  103.6 7.2 %all-to-all-done.2 = f32[8,16,2,128,4]{3,1,4,2,0:T(8,128)S(1)} async-done(((f32[8,16,2,128,4]{3,1,4,2,0:T(8,128)}), f32[8,16,2,128,4]{3,1,4,2,0:T(8,128)S(1)}, u32[]{:S(2)}, u32[]{:S(2)}) %all-to-all-start.2) | async-done | bytes 524320 | tf_op jit(solution)/shard_map/all_to_all | solution.py:86
  110.8 1.4 copy.74
  112.2 0.5 copy.75
  112.8 0.0 copy-start
  112.8 4.9 %fusion.21 = f32[128,32,32]{2,1,0:T(8,128)S(1)} fusion(f32[16,128,32]{2,0,1:T(8,128)S(1)} %copy.64, f32[16,1,128,32]{3,0,2,1:T(8,128)} %copy.74), kind=kOutput, calls=%fused_computation.28 | convolution fusion | flops 25165824 | bytes 1048576 | tf_op jit(solution)/shard_map/wfs,wfc->fsc/dot_general | solution.py:92
  117.7 0.0 copy-done
  117.7 3.6 %fusion.19 = f32[128,32,32]{2,1,0:T(8,128)S(1)} fusion(f32[16,128,32]{2,0,1:T(8,128)S(1)} %copy.66, f32[16,1,128,32]{3,0,2,1:T(8,128)S(1)} %copy-done), kind=kOutput, calls=%fused_computation.26 | convolution fusion | flops 25165824 | bytes 1048576 | tf_op jit(solution)/shard_map/wfs,wfc->fsc/dot_general | solution.py:95
  121.4 3.9 %add_bitcast_fusion = f32[1,128,32,32]{3,2,1,0:T(8,128)S(1)} fusion(f32[128,32,32]{2,1,0:T(8,128)S(1)} %fusion.21, f32[16,128,32]{2,0,1:T(8,128)S(1)} %copy.66, f32[16,1,128,32]{3,0,2,1:T(8,128)S(1)} %copy.75), kind=kOutput, calls=%fused_computation.14 | convolution fusion | flops 25296896 | bytes 1572864 | tf_op jit(solution)/shard_map/wfs,wfc->fsc/dot_general | solution.py:94
  125.3 3.7 %subtract_bitcast_fusion = f32[1,128,32,32]{3,2,1,0:T(8,128)S(1)} fusion(f32[128,32,32]{2,1,0:T(8,128)S(1)} %fusion.19, f32[16,128,32]{2,0,1:T(8,128)S(1)} %copy.64, f32[16,1,128,32]{3,0,2,1:T(8,128)S(1)} %copy.75), kind=kOutput, calls=%fused_computation.13 | convolution fusion | flops 25296896 | bytes 1572864 | tf_op jit(solution)/shard_map/wfs,wfc->fsc/dot_general | solution.py:97
  129.0 0.0 copy-start.1
  129.0 0.6 pad_maximum_fusion
  129.6 0.3 copy-done.1
  129.9 9.1 %fusion.11 = f32[32,256,32]{1,2,0:T(8,128)} fusion(f32[2,128,32,32]{3,2,1,0:T(8,128)S(1)} %pad_maximum_fusion, f32[256,1,128]{2,0,1:T(8,128)S(1)} %copy-done.1, f32[256,1,128]{2,0,1:T(8,128)S(1)} %get-tuple-element.11), kind=kOutput, calls=%fused_computation.19 | convolution fusion | flops 805371904 | bytes 2359296 | tf_op jit(solution)/shard_map/tak,aksc->stc/dot_general | solution.py:105
  139.0 0.0 reduce-scatter.2.cloned.1.call-update
  139.1 24.7 %reduce-scatter.2.cloned.1.call-done = f32[8,256,32]{1,2,0:T(8,128)} async-done(((f32[32,256,32]{1,2,0:T(8,128)}), f32[8,256,32]{1,2,0:T(8,128)}) %reduce-scatter.2.cloned.1.call-update) | async-done | bytes 262160 | tf_op jit(solution)/shard_map/reduce_scatter | solution.py:104
  (13 shorter events, 0.3 us)
Async XLA Ops:
  8.6 14.9 %all-to-all-start = ((f32[4,128,256]{1,0,2:T(4,128)}), f32[4,128,256]{1,0,2:T(4,128)S(1)}, u32[]{:S(2)}, u32[]{:S(2)}) async-start(f32[4,128,256]{1,0,2:T(4,128)} %copy.54), calls=%async_computation | async-start | bytes 1048576 | tf_op jit(solution)/shard_map/all_to_all | solution.py:58
  69.9 6.9 %copy-start.2 = (s32[32]{0:T(128)S(1)}, s32[32]{0:T(128)}, u32[]{:S(2)}) copy-start(s32[32]{0:T(128)} %param.3) | copy-start | bytes 388
  72.0 19.5 %all-to-all-start.1 = ((f32[4,1,32768]{2,1,0:T(1,128)}), f32[4,1,32768]{2,1,0:T(1,128)S(1)}, u32[]{:S(2)}, u32[]{:S(2)}) async-start(f32[4,1,32768]{2,1,0:T(1,128)} %reshape.211), calls=%async_computation.1 | async-start | bytes 1048576 | tf_op jit(solution)/shard_map/all_to_all | solution.py:72
  97.2 13.5 %all-to-all-start.2 = ((f32[8,16,2,128,4]{3,1,4,2,0:T(8,128)}), f32[8,16,2,128,4]{3,1,4,2,0:T(8,128)S(1)}, u32[]{:S(2)}, u32[]{:S(2)}) async-start(f32[8,16,2,128,4]{3,1,4,2,0:T(8,128)} %stack.32), calls=%async_computation.2 | async-start | bytes 1048576 | tf_op jit(solution)/shard_map/all_to_all | solution.py:86
  101.0 62.7 %reduce-scatter.2.cloned.1.call-start = ((), (), s32[]{:S(2)}) async-start(), calls=%async_computation.4 | async-start | bytes 1310720 | tf_op jit(solution)/shard_map/reduce_scatter | solution.py:104
  112.8 4.9 %copy-start = (f32[16,1,128,32]{3,0,2,1:T(8,128)S(1)}, f32[16,1,128,32]{3,0,2,1:T(8,128)}, u32[]{:S(2)}) copy-start(f32[16,1,128,32]{3,0,2,1:T(8,128)} %copy.74) | copy-start | bytes 786436
  129.0 0.9 copy-start.1
Sparse Core Ops, SparseCore 0:
  139.2 24.5 reduce-scatter.1
